TPU v7x, 32 devices: a whole 2x2x4 slice. The times are simulated.
32 devices in a mesh: fsdp: 32 (over z, y, x, core).
Axes of the slice: x: 2, y: 2, z: 4, core: 2. Of those that a mesh axis runs over, the one named last changes fastest.
Arguments:
- hidden_in: bfloat16 [2, 32768, 768], P(None, 'fsdp'), may hold values from -26 to 26
- doc_lens: int32 [2, 32, 2], P(None, 'fsdp'), may hold values from 1 to 768, 1024 in all within a row
- w_qkv: bfloat16 [1769472], P('fsdp'), may hold values from -0.21875 to 0.21875
- w_out: bfloat16 [589824], P('fsdp'), may hold values from -0.21875 to 0.21875
- w_fc1: bfloat16 [2359296], P('fsdp'), may hold values from -0.21875 to 0.21875
- w_fc2: bfloat16 [2359296], P('fsdp'), may hold values from -0.109375 to 0.109375
- vec_params: bfloat16 [16896], P('fsdp'), may hold values from -1.5 to 1.5
- cotangent: bfloat16 [2, 32768, 768], P(None, 'fsdp'), may hold values from -6 to 6
Outputs:
- hidden_out: bfloat16 [2, 32768, 768], P(None, 'fsdp')
- input_grad: bfloat16 [2, 32768, 768], P(None, 'fsdp')
- grad_qkv: float32 [1769472], P('fsdp')
- grad_out: float32 [589824], P('fsdp')
- grad_fc1: float32 [2359296], P('fsdp')
- grad_fc2: float32 [2359296], P('fsdp')
- grad_vec: float32 [16896], P('fsdp')
Inputs may be any that keep to these rules, and one draw needn't show every extreme that they name: `doc_lens`: the 2 lengths of one sequence sum to 1024.
All inputs are finite; a program needn't handle non-finite values.
Results may differ from a plain program's by a relative error of at most 0.008.
Values may be sent and summed in bfloat16 or wider, within the bound.
No kernel may reach another device: no remote copies, remote signals or barrier semaphores. Data moves between devices by JAX's collectives and lax.ppermute only.
A program may use at most 448 MiB of HBM per device.

v0:
```python
import jax
import jax.numpy as jnp
from jax import lax
from jax.sharding import PartitionSpec as P

HEADS = 12
HEAD_DIM = 64
BLOCK = 256


EPSILON = 1e-05
MASKED_SCORE = -1e30


def layer_norm(inputs, factor, offset):
    average = jnp.mean(inputs, axis=-1, keepdims=True)
    centred = inputs - average
    variance = jnp.mean(centred * centred, axis=-1, keepdims=True)
    return centred * lax.rsqrt(variance + EPSILON) * factor + offset


def ffn_inner(preact_in, factor, offset):
    return layer_norm(jax.nn.gelu(preact_in, approximate=False), factor, offset)


def visible_mask(lengths, seq_len):
    places = jnp.arange(seq_len, dtype=jnp.int32)
    doc_ends = jnp.cumsum(lengths)
    doc_starts = doc_ends - lengths
    doc_index = jnp.sum((places[:, None] >= doc_ends[None, :]).astype(jnp.int32), axis=1)
    member = doc_index[:, None] == jnp.arange(lengths.shape[0], dtype=jnp.int32)[None, :]
    doc_first = jnp.sum(jnp.where(member, doc_starts[None, :], 0), axis=1)
    block_index = (places - doc_first) // BLOCK
    same_doc = doc_index[:, None] == doc_index[None, :]
    return same_doc & (block_index[None, :] <= block_index[:, None])


def split_vector(vector, model_width, hidden):
    sizes_list = [model_width] * 9 + [hidden] * 3 + [model_width]
    pieces = []
    offset = 0
    for length in sizes_list:
        pieces.append(vector[offset : offset + length])
        offset += length
    return pieces


def block_scores(block_q, key_heads, visible_rows, score_scale):
    scores = (
        jnp.einsum("qhd,khd->hqk", block_q, key_heads, preferred_element_type=jnp.float32)
        * score_scale
    )
    return jnp.where(visible_rows[None], scores, MASKED_SCORE)


def attend_forward(query_heads, key_heads, value_heads, visible, score_scale):
    seq_len = query_heads.shape[0]
    block_rows = min(512, seq_len)
    outputs = []
    log_sums = []
    for row_start in range(0, seq_len, block_rows):
        scores = block_scores(
            query_heads[row_start : row_start + block_rows],
            key_heads,
            visible[row_start : row_start + block_rows],
            score_scale,
        )
        row_top = jnp.max(scores, axis=-1, keepdims=True)
        exponent = jnp.exp(scores - row_top)
        totals = jnp.sum(exponent, axis=-1, keepdims=True)
        probabilities = (exponent / totals).astype(jnp.bfloat16)
        outputs.append(
            jnp.einsum(
                "hqk,khd->qhd", probabilities, value_heads, preferred_element_type=jnp.float32
            )
        )
        log_sums.append(row_top + jnp.log(totals))
    return (jnp.concatenate(outputs, axis=0), log_sums)


def attend_backward(
    query_heads, key_heads, value_heads, visible, score_scale, log_sums, grad_heads
):
    seq_len = query_heads.shape[0]
    block_rows = min(512, seq_len)
    grad_q_list = []
    grad_k = jnp.zeros(key_heads.shape, jnp.float32)
    grad_v = jnp.zeros(value_heads.shape, jnp.float32)
    for block_number, row_start in enumerate(range(0, seq_len, block_rows)):
        block_q = query_heads[row_start : row_start + block_rows]
        scores = block_scores(
            block_q, key_heads, visible[row_start : row_start + block_rows], score_scale
        )
        probabilities = jnp.exp(scores - log_sums[block_number])
        block_do = grad_heads[row_start : row_start + block_rows]
        grad_p = jnp.einsum(
            "qhd,khd->hqk", block_do, value_heads, preferred_element_type=jnp.float32
        )
        inner_sum = jnp.sum(grad_p * probabilities, axis=-1, keepdims=True)
        grad_s = (probabilities * (grad_p - inner_sum)).astype(jnp.bfloat16) * score_scale
        grad_q_list.append(
            jnp.einsum("hqk,khd->qhd", grad_s, key_heads, preferred_element_type=jnp.float32)
        )
        grad_k = grad_k + jnp.einsum(
            "hqk,qhd->khd", grad_s, block_q, preferred_element_type=jnp.float32
        )
        grad_v = grad_v + jnp.einsum(
            "hqk,qhd->khd",
            probabilities.astype(jnp.bfloat16),
            block_do,
            preferred_element_type=jnp.float32,
        )
    return (jnp.concatenate(grad_q_list, axis=0), grad_k, grad_v)


def add_tuples(totals, extra):
    if totals is None:
        return extra
    return jax.tree.map(lambda first_arr, second_arr: first_arr + second_arr, totals, extra)


def shards(hidden_in, doc_lens, w_qkv, w_out, w_fc1, w_fc2, vec_params, cotangent):
    micro_count, seq_len, model_width = hidden_in.shape
    score_scale = HEAD_DIM ** (-0.5)
    outputs_list = []
    input_grads = []
    accumulated = None
    for micro_index in range(micro_count):
        attn_flat = (
            lax.all_gather(w_qkv, "fsdp", axis=0, tiled=True),
            lax.all_gather(w_out, "fsdp", axis=0, tiled=True),
            lax.all_gather(vec_params, "fsdp", axis=0, tiled=True),
        )
        ffn_flat = (
            lax.all_gather(w_fc1, "fsdp", axis=0, tiled=True),
            lax.all_gather(w_fc2, "fsdp", axis=0, tiled=True),
        )
        hidden = ffn_flat[0].shape[0] // model_width
        mat_qkv = attn_flat[0].reshape(model_width, 3 * model_width)
        mat_out = attn_flat[1].reshape(model_width, model_width)
        vector = attn_flat[2].astype(jnp.float32)
        mat_fc1 = ffn_flat[0].reshape(model_width, hidden)
        mat_fc2 = ffn_flat[1].reshape(hidden, model_width)
        (
            ln1_gain,
            ln1_bias,
            q_bias,
            v_bias,
            attn_gain,
            attn_bias,
            out_bias,
            ln2_gain,
            ln2_bias,
            fc1_bias,
            ffn_gain,
            ffn_bias,
            fc2_bias,
        ) = split_vector(vector, model_width, hidden)
        inputs = hidden_in[micro_index].astype(jnp.float32)
        visible = visible_mask(doc_lens[micro_index, 0], seq_len)
        normed = layer_norm(inputs, ln1_gain, ln1_bias).astype(jnp.bfloat16)
        projected = jnp.dot(normed, mat_qkv, preferred_element_type=jnp.float32)
        query_heads = (
            (projected[:, :model_width] + q_bias)
            .astype(jnp.bfloat16)
            .reshape(seq_len, HEADS, HEAD_DIM)
        )
        key_heads = (
            projected[:, model_width : 2 * model_width]
            .astype(jnp.bfloat16)
            .reshape(seq_len, HEADS, HEAD_DIM)
        )
        value_heads = (
            (projected[:, 2 * model_width :] + v_bias)
            .astype(jnp.bfloat16)
            .reshape(seq_len, HEADS, HEAD_DIM)
        )
        attended, log_sums = attend_forward(
            query_heads, key_heads, value_heads, visible, score_scale
        )
        attended = attended.reshape(seq_len, model_width)
        mixed_rows = layer_norm(attended, attn_gain, attn_bias).astype(jnp.bfloat16)
        after_attn = (
            inputs + jnp.dot(mixed_rows, mat_out, preferred_element_type=jnp.float32) + out_bias
        )
        normed_two = layer_norm(after_attn, ln2_gain, ln2_bias).astype(jnp.bfloat16)
        preact = jnp.dot(normed_two, mat_fc1, preferred_element_type=jnp.float32) + fc1_bias
        inner_rows = ffn_inner(preact, ffn_gain, ffn_bias).astype(jnp.bfloat16)
        result = (
            after_attn + jnp.dot(inner_rows, mat_fc2, preferred_element_type=jnp.float32) + fc2_bias
        )
        outputs_list.append(result.astype(jnp.bfloat16))
        regathered = (
            lax.all_gather(w_qkv, "fsdp", axis=0, tiled=True),
            lax.all_gather(w_out, "fsdp", axis=0, tiled=True),
            lax.all_gather(w_fc1, "fsdp", axis=0, tiled=True),
            lax.all_gather(w_fc2, "fsdp", axis=0, tiled=True),
            lax.all_gather(vec_params, "fsdp", axis=0, tiled=True),
        )
        back_qkv = regathered[0].reshape(model_width, 3 * model_width)
        back_out = regathered[1].reshape(model_width, model_width)
        back_fc1 = regathered[2].reshape(model_width, hidden)
        back_fc2 = regathered[3].reshape(hidden, model_width)
        back_vector = regathered[4].astype(jnp.float32)
        (
            ln1_gain_b,
            ln1_bias_b,
            q_bias_b,
            v_bias_b,
            attn_gain_b,
            attn_bias_b,
            out_bias_b,
            ln2_gain_b,
            ln2_bias_b,
            fc1_bias_b,
            ffn_gain_b,
            ffn_bias_b,
            fc2_bias_b,
        ) = split_vector(back_vector, model_width, hidden)
        cot_rows = cotangent[micro_index]
        cot_float = cot_rows.astype(jnp.float32)
        grad_c2 = jnp.sum(cot_float, axis=0)
        grad_fc2 = jnp.einsum("sf,sd->fd", inner_rows, cot_rows, preferred_element_type=jnp.float32)
        grad_inner = jnp.einsum("sd,fd->sf", cot_rows, back_fc2, preferred_element_type=jnp.float32)
        ignored_ffn, ffn_pull = jax.vjp(ffn_inner, preact, ffn_gain_b, ffn_bias_b)
        grad_pre, grad_ffn_gain, grad_ffn_bias = ffn_pull(grad_inner)
        grad_pre_low = grad_pre.astype(jnp.bfloat16)
        grad_c1 = jnp.sum(grad_pre_low, axis=0, dtype=jnp.float32)
        grad_fc1 = jnp.einsum(
            "sd,sf->df", normed_two, grad_pre_low, preferred_element_type=jnp.float32
        )
        grad_normed_two = jnp.einsum(
            "sf,df->sd", grad_pre_low, back_fc1, preferred_element_type=jnp.float32
        )
        ignored_two, ln2_pull = jax.vjp(layer_norm, after_attn, ln2_gain_b, ln2_bias_b)
        grad_after, grad_ln2_gain, grad_ln2_bias = ln2_pull(grad_normed_two)
        grad_after = grad_after + cot_float
        grad_after_low = grad_after.astype(jnp.bfloat16)
        grad_bo = jnp.sum(grad_after_low, axis=0, dtype=jnp.float32)
        grad_wo = jnp.einsum(
            "sd,se->de", mixed_rows, grad_after_low, preferred_element_type=jnp.float32
        )
        grad_mixed = jnp.einsum(
            "se,de->sd", grad_after_low, back_out, preferred_element_type=jnp.float32
        )
        ignored_attn, attn_pull = jax.vjp(layer_norm, attended, attn_gain_b, attn_bias_b)
        grad_attended, grad_attn_gain, grad_attn_bias = attn_pull(grad_mixed)
        grad_heads = grad_attended.astype(jnp.bfloat16).reshape(seq_len, HEADS, HEAD_DIM)
        grad_q, grad_k, grad_v = attend_backward(
            query_heads, key_heads, value_heads, visible, score_scale, log_sums, grad_heads
        )
        grad_qkv_rows = jnp.concatenate(
            [
                grad_q.reshape(seq_len, model_width),
                grad_k.reshape(seq_len, model_width),
                grad_v.reshape(seq_len, model_width),
            ],
            axis=1,
        ).astype(jnp.bfloat16)
        grad_bq = jnp.sum(grad_qkv_rows[:, :model_width], axis=0, dtype=jnp.float32)
        grad_bv = jnp.sum(grad_qkv_rows[:, 2 * model_width :], axis=0, dtype=jnp.float32)
        grad_wqkv = jnp.einsum(
            "sd,se->de", normed, grad_qkv_rows, preferred_element_type=jnp.float32
        )
        grad_normed = jnp.einsum(
            "se,de->sd", grad_qkv_rows, back_qkv, preferred_element_type=jnp.float32
        )
        ignored_one, ln1_pull = jax.vjp(layer_norm, inputs, ln1_gain_b, ln1_bias_b)
        grad_inputs, grad_ln1_gain, grad_ln1_bias = ln1_pull(grad_normed)
        input_grads.append((grad_after + grad_inputs).astype(jnp.bfloat16))
        grad_vector = jnp.concatenate(
            [
                grad_ln1_gain,
                grad_ln1_bias,
                grad_bq,
                grad_bv,
                grad_attn_gain,
                grad_attn_bias,
                grad_bo,
                grad_ln2_gain,
                grad_ln2_bias,
                grad_c1,
                grad_ffn_gain,
                grad_ffn_bias,
                grad_c2,
            ]
        )
        flat_qkv = grad_wqkv.reshape(-1)
        flat_out = grad_wo.reshape(-1)
        flat_fc1 = grad_fc1.reshape(-1)
        flat_fc2 = grad_fc2.reshape(-1)
        shares = (
            lax.psum_scatter(flat_qkv, "fsdp", scatter_dimension=0, tiled=True),
            lax.psum_scatter(flat_out, "fsdp", scatter_dimension=0, tiled=True),
            lax.psum_scatter(flat_fc1, "fsdp", scatter_dimension=0, tiled=True),
            lax.psum_scatter(flat_fc2, "fsdp", scatter_dimension=0, tiled=True),
            lax.psum_scatter(grad_vector, "fsdp", scatter_dimension=0, tiled=True),
        )
        accumulated = add_tuples(accumulated, tuple(shares))
    hidden_out = jnp.stack(outputs_list, axis=0)
    input_grad = jnp.stack(input_grads, axis=0)
    return (
        hidden_out,
        input_grad,
        accumulated[0],
        accumulated[1],
        accumulated[2],
        accumulated[3],
        accumulated[4],
    )


def solution(mesh):
    return jax.shard_map(
        shards,
        mesh=mesh,
        in_specs=(
            P(None, "fsdp", None),
            P(None, "fsdp", None),
            P("fsdp"),
            P("fsdp"),
            P("fsdp"),
            P("fsdp"),
            P("fsdp"),
            P(None, "fsdp", None),
        ),
        out_specs=(
            P(None, "fsdp", None),
            P(None, "fsdp", None),
            P("fsdp"),
            P("fsdp"),
            P("fsdp"),
            P("fsdp"),
            P("fsdp"),
        ),
        check_vma=False,
    )
```

profile of v0, /device:TPU:0, one launch (start us, length us, event | category | flops | bytes accessed | tf_op | source)
XLA Modules:
  0.0 1667.8 jit_solution(589054889296489579)
XLA Ops:
  10.9 42.4 %all-reduce = bf16[16896]{0:T(1024)(128)(2,1)S(1)} all-reduce(bf16[16896]{0:T(1024)(128)(2,1)S(1)} %dynamic-update-slice), channel_id=1, replica_groups=mesh['fsdp'=32] {'fsdp'}, use_global_device_ids=true, to_apply=%add | all-reduce | flops 16896 | bytes 67584
  78.0 51.7 %all-gather.5.cloned.1.call-done = bf16[1769472]{0:T(1024)(128)(2,1)} async-done(((bf16[55296]{0:T(1024)(128)(2,1)}), bf16[1769472]{0:T(1024)(128)(2,1)}) %all-gather.5.cloned.1.call-update) | async-done | bytes 3538960 | tf_op jit(solution)/shard_map/all_gather | solution.py:130
  129.7 8.0 reshape.681
  137.8 6.5 fusion.200
  144.4 4.3 fusion.203
  161.0 12.7 fusion.13
  173.6 12.8 fusion.9
  189.9 8.5 fusion.69
  200.8 12.0 fusion.12
  212.8 12.4 fusion.8
  228.4 8.5 fusion.68
  245.1 12.9 fusion.15
  258.0 12.5 fusion.11
  273.6 8.5 fusion.71
  284.4 12.1 fusion.14
  296.5 12.3 fusion.10
  311.9 10.0 fusion.70
  322.6 5.8 pad_maximum_fusion.2
  338.7 8.2 reshape.687
  347.0 7.7 fusion.378
  354.7 70.3 %fusion.387 = (f32[1024]{0:T(1024)S(1)}, f32[1024,3072]{1,0:T(8,128)}, f32[1024,3072]{1,0:T(8,128)}, f32[1024]{0:T(1024)S(1)}, f32[1024,3072]{1,0:T(8,128)}, /*index=5*/f32[1024,3072]{1,0:T(8,128)}, f32[1024,3072]{1,0:T(8,128)}) fusion(f32[3072]{0:T(1024)S(1)} %copy-done.112, f32[1024,3072]{1,0:T(8,128)S(1)} %fusion.378, ...), kind=kOutput, calls=%fused_computation.486 | convolution fusion | flops 5247072256 | bytes 81809408 | tf_op jit(solution)/shard_map/dot_general | solution.py:187
  425.1 9.5 reshape.688
  434.5 10.5 fusion.208
  445.0 19.9 %multiply_reduce_fusion.7 = (f32[1024]{0:T(1024)S(1)}, f32[1024]{0:T(1024)S(1)}, f32[3072]{0:T(1024)}, f32[3072]{0:T(1024)}, f32[1024]{0:T(1024)S(1)}, /*index=5*/f32[1024]{0:T(1024)S(1)}, f32[1024,3072]{1,0:T(8,128)}) fusion(f32[1024,3072]{1,0:T(8,128)} %get-tuple-element.86, f32[3072]{0:T(1024)S(1)} %copy-done.90, f32[1024]{0:T(1024)S(1)} %broadcast_multiply_fusion.1, ...), kind=kOutput, calls=%fused_computation.61 | convolution fusion | flops 4875868160 | bytes 56684544 | tf_op jit(solution)/shard_map/sd,fd->sf/dot_general | solution.py:224
  464.9 18.6 %multiply_reduce_fusion.5 = (f32[3072]{0:T(1024)}, f32[1024]{0:T(1024)S(1)}, f32[1024]{0:T(1024)S(1)}, f32[3072]{0:T(1024)}) fusion(f32[1024,3072]{1,0:T(8,128)} %get-tuple-element.177, f32[1024,3072]{1,0:T(8,128)} %get-tuple-element.86, f32[1024]{0:T(1024)S(1)} %get-tuple-element.157, f32[1024]{0:T(1024)S(1)} %broadcast_multiply_fusion.1, ...), kind=kLoop, calls=%fused_computation.52 | loop fusion | flops 62906368 | bytes 50401280 | tf_op jit(solution)/shard_map/transpose(jvp())/reduce_sum | solution.py:19
  483.5 45.3 %convert_reduce_fusion = (f32[3072]{0:T(1024)}, bf16[1024,3072]{1,0:T(8,128)(2,1)}, bf16[1024,3072]{1,0:T(8,128)(2,1)}, bf16[1024,3072]{1,0:T(8,128)(2,1)}, f32[3072]{0:T(1024)}, /*index=5*/bf16[1024,3072]{1,0:T(8,128)(2,1)}) fusion(f32[1024,3072]{1,0:T(8,128)} %get-tuple-element.140, f32[1024]{0:T(1024)S(1)} %negate_multiply_fusion.5, ...), kind=kLoop, calls=%fused_computation.51 | loop fusion | flops 176154624 | bytes 125923328 | tf_op jit(solution)/shard_map/reduce_sum | solution.py:228
  528.9 9.2 fusion.402
  540.4 10.4 fusion.404
  550.9 3.7 copy.119
  554.7 5.4 multiply_reduce_fusion.12
  572.8 4.9 multiply_reduce_fusion.13
  581.8 10.1 fusion.406
  592.0 13.3 fusion.56
  605.3 52.7 %fusion.96 = f32[12,64,1024]{2,1,0:T(8,128)} fusion(bf16[512,12,64]{0,2,1:T(8,128)(2,1)S(1)} %bitcast.319, f32[12,512,1024]{2,1,0:T(8,128)} %fusion.406, f32[12,512,1024]{2,1,0:T(8,128)} %get-tuple-element.169, f32[12,512]{1,0:T(8,128)S(1)} %copy-done.143, pred[512,1024]{1,0:T(8,128)(4,1)S(1)} %copy-done.61), kind=kOutput, calls=%fused_computation.126 | convolution fusion | flops 893393920 | bytes 54812672 | tf_op jit(solution)/shard_map/hqk,qhd->khd/dot_general | solution.py:104
  657.9 52.2 %fusion.270 = bf16[512,12,64]{0,2,1:T(8,128)(2,1)} fusion(bf16[1024,12,64]{0,2,1:T(8,128)(2,1)} %bitcast.284, f32[12,512,1024]{2,1,0:T(8,128)} %fusion.406, f32[12,512,1024]{2,1,0:T(8,128)} %get-tuple-element.169, f32[12,512]{1,0:T(8,128)S(1)} %copy-done.143, pred[512,1024]{1,0:T(8,128)(4,1)} %get-tuple-element.117), kind=kOutput, calls=%fused_computation.314 | convolution fusion | flops 893787136 | bytes 53239808 | tf_op jit(solution)/shard_map/hqk,khd->qhd/dot_general | solution.py:102
  712.5 10.2 fusion.408
  722.6 13.0 fusion.52
  735.7 54.2 %fusion.72 = f32[12,64,1024]{2,1,0:T(8,128)} fusion(bf16[512,12,64]{0,2,1:T(8,128)(2,1)} %bitcast.321, f32[12,512,1024]{2,1,0:T(8,128)} %fusion.408, f32[12,512,1024]{2,1,0:T(8,128)} %get-tuple-element.165, f32[12,512]{1,0:T(8,128)S(1)} %copy-done.144, pred[512,1024]{1,0:T(8,128)(4,1)} %get-tuple-element.119), kind=kOutput, calls=%fused_computation.118 | convolution fusion | flops 893393920 | bytes 54812672 | tf_op jit(solution)/shard_map/hqk,qhd->khd/dot_general | solution.py:104
  789.9 52.0 %fusion.260 = bf16[512,12,64]{0,2,1:T(8,128)(2,1)} fusion(bf16[1024,12,64]{0,2,1:T(8,128)(2,1)} %bitcast.280, f32[12,512,1024]{2,1,0:T(8,128)} %fusion.408, f32[12,512,1024]{2,1,0:T(8,128)} %get-tuple-element.165, f32[12,512]{1,0:T(8,128)S(1)} %copy-done.144, pred[512,1024]{1,0:T(8,128)(4,1)} %get-tuple-element.119), kind=kOutput, calls=%fused_computation.312 | convolution fusion | flops 893787136 | bytes 53239808 | tf_op jit(solution)/shard_map/hqk,khd->qhd/dot_general | solution.py:102
  841.9 11.6 fusion.405
  853.5 13.1 add_convert_fusion.11
  866.7 51.6 %fusion.275 = bf16[512,12,64]{0,2,1:T(8,128)(2,1)} fusion(bf16[1024,12,64]{0,2,1:T(8,128)(2,1)S(1)} %bitcast.285, f32[12,512,1024]{2,1,0:T(8,128)} %fusion.405, f32[12,512,1024]{2,1,0:T(8,128)} %get-tuple-element.171, f32[12,512]{1,0:T(8,128)S(1)} %copy-done.142, pred[512,1024]{1,0:T(8,128)(4,1)} %get-tuple-element.116), kind=kOutput, calls=%fused_computation.315 | convolution fusion | flops 893787136 | bytes 53239808 | tf_op jit(solution)/shard_map/hqk,khd->qhd/dot_general | solution.py:102
  918.3 48.2 %add_convert_fusion.12 = bf16[12,64,1024]{2,1,0:T(8,128)(2,1)} fusion(f32[12,64,1024]{2,1,0:T(8,128)} %fusion.96, bf16[512,12,64]{0,2,1:T(8,128)(2,1)} %bitcast.317, f32[12,512,1024]{2,1,0:T(8,128)} %fusion.405, f32[12,512,1024]{2,1,0:T(8,128)} %get-tuple-element.171, f32[12,512]{1,0:T(8,128)S(1)} %copy-done.142, pred[512,1024]{1,0:T(8,128)(4,1)} %get-tuple-element.116), kind=kOutput, calls=%fused_computation.249 | convolution fusion | flops 894966784 | bytes 56385536 | tf_op jit(solution)/shard_map/hqk,qhd->khd/dot_general | solution.py:104
  966.8 9.2 fusion.401
  976.2 6.9 fusion.181
  983.2 7.7 fusion.376
  997.5 11.9 fusion.407
  1009.4 13.0 add_convert_fusion.7
  1022.4 51.9 %fusion.265 = bf16[512,12,64]{0,2,1:T(8,128)(2,1)} fusion(bf16[1024,12,64]{0,2,1:T(8,128)(2,1)S(1)} %bitcast.281, f32[12,512,1024]{2,1,0:T(8,128)} %fusion.407, f32[12,512,1024]{2,1,0:T(8,128)} %get-tuple-element.167, f32[12,512]{1,0:T(8,128)S(1)} %copy-done.141, pred[512,1024]{1,0:T(8,128)(4,1)} %get-tuple-element.118), kind=kOutput, calls=%fused_computation.313 | convolution fusion | flops 893787136 | bytes 53239808 | tf_op jit(solution)/shard_map/hqk,khd->qhd/dot_general | solution.py:102
  1074.3 48.2 %add_convert_fusion.8 = bf16[12,64,1024]{2,1,0:T(8,128)(2,1)} fusion(f32[12,64,1024]{2,1,0:T(8,128)} %fusion.72, bf16[512,12,64]{0,2,1:T(8,128)(2,1)} %bitcast.315, f32[12,512,1024]{2,1,0:T(8,128)} %fusion.407, f32[12,512,1024]{2,1,0:T(8,128)} %get-tuple-element.167, f32[12,512]{1,0:T(8,128)S(1)} %copy-done.141, pred[512,1024]{1,0:T(8,128)(4,1)} %get-tuple-element.118), kind=kOutput, calls=%fused_computation.243 | convolution fusion | flops 894966784 | bytes 56385536 | tf_op jit(solution)/shard_map/hqk,qhd->khd/dot_general | solution.py:104
  1126.1 5.5 fusion.403
  1131.6 3.6 copy.120
  1135.3 4.2 fusion.148
  1140.9 5.5 convert_reduce_fusion.5
  1149.4 7.1 convolution_add_fusion
  1156.5 8.2 reshape.709
  1172.7 9.8 add_bitcast_fusion
  1182.5 5.9 copy.133
  1188.4 7.7 fusion.210
  1196.1 7.8 convolution_add_fusion.1
  1204.1 10.8 reshape.712
  1216.8 8.8 fusion.239
  1225.6 8.9 fusion.238
  1242.5 410.4 %all-reduce.9.cloned.1.call-done = (f32[1769472]{0:T(1024)}, f32[589824]{0:T(1024)}, f32[2359296]{0:T(1024)}, f32[2359296]{0:T(1024)}, f32[16896]{0:T(1024)}) async-done(((f32[1769472]{0:T(1024)}, f32[589824]{0:T(1024)}, f32[2359296]{0:T(1024)}, f32[2359296]{0:T(1024)}, f32[16896]{0:T(1024)}), (f32[1769472]{0:T(1024)}, f32[589824]{0:T(1024)}, f32[2359296]{0:T(1024)}, f32[2359296]{0:T(1024)}, ...) | async-done | bytes 28379152
  (510 shorter events, 138.4 us)
Async XLA Ops:
  7.2 67.5 %all-gather.7.cloned.1.call-start = ((), (), s32[]{:S(2)}) async-start(), calls=%async_computation.1 | async-start | bytes 1216512 | tf_op jit(solution)/shard_map/all_gather | solution.py:131
  7.9 121.8 %all-gather.5.cloned.1.call-start = ((), (), s32[]{:S(2)}) async-start(), calls=%async_computation | async-start | bytes 3649536 | tf_op jit(solution)/shard_map/all_gather | solution.py:130
  8.6 330.0 %all-gather.9.cloned.1.call-start = ((), (), s32[]{:S(2)}) async-start(), calls=%async_computation.2 | async-start | bytes 4866048 | tf_op jit(solution)/shard_map/all_gather | solution.py:135
  9.4 415.7 %all-gather.11.cloned.1.call-start = ((), (), s32[]{:S(2)}) async-start(), calls=%async_computation.3 | async-start | bytes 4866048 | tf_op jit(solution)/shard_map/all_gather | solution.py:136
  10.0 1643.0 %all-reduce.9.cloned.1.call-start = ((), (), s32[]{:S(2)}) async-start(), calls=%async_computation.4 | async-start | bytes 56762368
  53.9 90.4 %copy-start.97 = (f32[768]{0:T(1024)}, f32[768]{0:T(1024)S(1)}, u32[]{:S(2)}) copy-start(f32[768]{0:T(1024)S(1)} %get-tuple-element.133) | copy-start | bytes 9220
  53.9 90.4 %copy-start.158 = (f32[768]{0:T(1024)}, f32[768]{0:T(1024)S(1)}, u32[]{:S(2)}) copy-start(f32[768]{0:T(1024)S(1)} %get-tuple-element.134) | copy-start | bytes 9220
  58.5 79.2 %copy-start.4 = (bf16[1,1024,768]{1,2,0:T(8,128)(2,1)}, bf16[1,1024,768]{1,2,0:T(8,128)(2,1)S(1)}, u32[]{:S(2)}) copy-start(bf16[1,1024,768]{1,2,0:T(8,128)(2,1)S(1)} %copy.130) | copy-start | bytes 4718596
  58.8 79.0 %copy-start.91 = (f32[1024]{0:T(1024)}, f32[1024]{0:T(1024)S(1)}, u32[]{:S(2)}) copy-start(f32[1024]{0:T(1024)S(1)} %broadcast_multiply_fusion.4) | copy-start | bytes 12292
  59.3 78.5 %copy-start.117 = (f32[1024]{0:T(1024)}, f32[1024]{0:T(1024)S(1)}, u32[]{:S(2)}) copy-start(f32[1024]{0:T(1024)S(1)} %fusion.294) | copy-start | bytes 12292
  61.0 83.3 %copy-start.7 = (bf16[1,1024,768]{1,2,0:T(8,128)(2,1)}, bf16[1,1024,768]{1,2,0:T(8,128)(2,1)S(1)}, u32[]{:S(2)}) copy-start(bf16[1,1024,768]{1,2,0:T(8,128)(2,1)S(1)} %copy.129) | copy-start | bytes 4718596
  61.3 83.0 %copy-start.99 = (f32[1024]{0:T(1024)}, f32[1024]{0:T(1024)S(1)}, u32[]{:S(2)}) copy-start(f32[1024]{0:T(1024)S(1)} %broadcast_multiply_fusion.7) | copy-start | bytes 12292
  62.4 82.0 %copy-start.119 = (f32[1024]{0:T(1024)}, f32[1024]{0:T(1024)S(1)}, u32[]{:S(2)}) copy-start(f32[1024]{0:T(1024)S(1)} %fusion.290) | copy-start | bytes 12292
  155.5 69.8 %copy-start.24 = (bf16[1024,768]{0,1:T(8,128)(2,1)}, bf16[1024,768]{0,1:T(8,128)(2,1)S(1)}, u32[]{:S(2)}) copy-start(bf16[1024,768]{0,1:T(8,128)(2,1)S(1)} %copy.104) | copy-start | bytes 4718596
  160.9 39.8 %copy-start.38 = (bf16[1024,768]{0,1:T(8,128)(2,1)}, bf16[1024,768]{0,1:T(8,128)(2,1)S(1)}, u32[]{:S(2)}) copy-start(bf16[1024,768]{0,1:T(8,128)(2,1)S(1)} %copy.106) | copy-start | bytes 4718596
  160.9 12.7 copy-start.60
  173.6 16.3 copy-start.2
  200.8 12.0 copy-start.58
  212.8 15.6 copy-start.1
  239.4 69.4 %copy-start.22 = (bf16[1024,768]{0,1:T(8,128)(2,1)}, bf16[1024,768]{0,1:T(8,128)(2,1)S(1)}, u32[]{:S(2)}) copy-start(bf16[1024,768]{0,1:T(8,128)(2,1)S(1)} %copy.110) | copy-start | bytes 4718596
  245.1 39.4 %copy-start.36 = (bf16[1024,768]{0,1:T(8,128)(2,1)}, bf16[1024,768]{0,1:T(8,128)(2,1)S(1)}, u32[]{:S(2)}) copy-start(bf16[1024,768]{0,1:T(8,128)(2,1)S(1)} %copy.112) | copy-start | bytes 4718596
  245.1 12.9 copy-start.56
  258.0 15.6 copy-start.3
  284.4 12.1 copy-start.54
  296.5 15.4 copy-start
  330.6 16.3 copy-start.11
  330.7 16.3 copy-start.82
  331.7 15.3 copy-start.85
  354.7 70.3 %copy-start.10 = (f32[1024,3072]{1,0:T(8,128)}, f32[1024,3072]{1,0:T(8,128)S(1)}, u32[]{:S(2)}) copy-start(f32[1024,3072]{1,0:T(8,128)S(1)} %fusion.378) | copy-start | bytes 37748740
  464.9 18.6 %copy-start.111 = (f32[3072]{0:T(1024)S(1)}, f32[3072]{0:T(1024)}, u32[]{:S(2)}) copy-start(f32[3072]{0:T(1024)} %get-tuple-element.123) | copy-start | bytes 36868
  592.0 13.3 copy-start.65
  657.9 54.5 %copy-start.23 = (bf16[1024,768]{0,1:T(8,128)(2,1)S(1)}, bf16[1024,768]{0,1:T(8,128)(2,1)}, u32[]{:S(2)}) copy-start(bf16[1024,768]{0,1:T(8,128)(2,1)} %copy-done.22) | copy-start | bytes 4718596
  841.9 11.6 copy-start.41
  841.9 11.6 copy-start.59
  841.9 11.6 copy-start.142
  841.9 11.6 copy-start.169
  853.5 13.1 copy-start.39
  918.3 48.2 %copy-start.77 = (bf16[512,12,64]{0,2,1:T(8,128)(2,1)S(1)}, bf16[512,12,64]{0,2,1:T(8,128)(2,1)}, u32[]{:S(2)}) copy-start(bf16[512,12,64]{0,2,1:T(8,128)(2,1)} %fusion.270) | copy-start | bytes 2359300
  918.3 48.2 %copy-start.78 = (bf16[512,12,64]{0,2,1:T(8,128)(2,1)S(1)}, bf16[512,12,64]{0,2,1:T(8,128)(2,1)}, u32[]{:S(2)}) copy-start(bf16[512,12,64]{0,2,1:T(8,128)(2,1)} %fusion.275) | copy-start | bytes 2359300
  966.8 16.3 slice-start.2
  997.4 11.9 copy-start.40
  997.5 11.9 copy-start.55
  997.5 11.9 copy-start.141
  997.5 11.9 copy-start.168
  1009.4 13.0 copy-start.37
  1074.3 50.3 %copy-start.71 = (bf16[12,64,1024]{2,1,0:T(8,128)(2,1)S(1)}, bf16[12,64,1024]{2,1,0:T(8,128)(2,1)}, u32[]{:S(2)}) copy-start(bf16[12,64,1024]{2,1,0:T(8,128)(2,1)} %add_convert_fusion.7) | copy-start | bytes 4718596
  1182.5 13.6 slice-start
  1204.0 11.0 copy-start.154
  1204.0 11.1 copy-start.153
  1204.0 11.1 copy-start.152
  1204.0 11.1 copy-start.150
  1204.0 11.1 copy-start.163
  1204.0 11.1 copy-start.114
  1204.0 11.1 copy-start.116
  1204.0 11.2 copy-start.156
  1204.0 11.2 copy-start.104
  1204.0 11.2 copy-start.151
  1204.0 11.2 copy-start.149
  1204.1 11.3 copy-start.148
  1204.1 11.3 copy-start.147
  1204.1 11.3 copy-start.162
  1204.1 11.3 copy-start.113
  1204.1 11.3 copy-start.115
  1204.1 11.3 copy-start.155
  (117 other events, 624.5 us)
Sparse Core Ops, SparseCore 0:
  10.9 56.8 all-gather.6
  70.7 58.9 all-gather.4
  132.6 62.4 all-gather.8
  197.9 62.4 all-gather.10
  1216.3 436.6 all-reduce.8
where the time goes:
time: 1680 us; the launch traced here: 1670 us
  matrix products  823 us (49%)
  waiting for transfers between devices  465 us (28%)
  other arithmetic  172 us (10%)
  local copies, waits for them, and re-layouts  149 us (9%)
  blocking collectives  42.4 us (3%)
    unnamed x6, waiting for transfers between devices  413 us
    dot_general x4, matrix products, attend_backward(): jnp.einsum('hqk,khd->qhd', grad_s, key_heads, preferred_element_type=jnp....  208 us
    dot_general x4, matrix products, attend_backward(): jnp.einsum('hqk,qhd->khd', grad_s, block_q, preferred_element_type=jnp.fl...  203 us
    dot_general x2, matrix products, shards(): jnp.dot(normed_two, mat_fc1, preferred_element_type=jnp.float32) + fc1_bias  78 us
    dot_general x4, matrix products, attend_backward(): jnp.einsum('hqk,qhd->khd', probabilities.astype(jnp.bfloat16), block_do,...  52.5 us
    all_gather x1, waiting for transfers between devices, shards(): lax.all_gather(w_qkv, 'fsdp', axis=0, tiled=True)  51.7 us
    unnamed x390, local copies, waits for them, and re-layouts  51.2 us
    reduce_sum x4, other arithmetic, attend_forward(): totals = jnp.sum(exponent, axis=-1, keepdims=True)  50 us
  transfers between devices with their start and end apart: 5, of which 2 were waited for; matrix products, arithmetic and copies ran while one was open for 20% of the time, Pallas kernels for 0%

commit v1 on v0

v1 whole, which is shorter than its diff:
```python
import functools

import jax
import jax.numpy as jnp
from jax import lax
from jax.experimental import pallas as pl
from jax.experimental.pallas import tpu as pltpu
from jax.sharding import PartitionSpec as P

HEADS = 12
HEAD_DIM = 64
BLOCK = 256

EPSILON = 1e-05
MASKED_SCORE = -1e30
BF = jnp.bfloat16
F32 = jnp.float32
TILE = 128
LIMIT = 64 * 1024 * 1024 - 1024 * 1024


def params(limit=LIMIT):
    return pltpu.CompilerParams(vmem_limit_bytes=limit)


def cost(flops, bytes_accessed, transcendentals=0):
    return pl.CostEstimate(
        flops=int(flops), bytes_accessed=int(bytes_accessed), transcendentals=int(transcendentals)
    )


def whole(shape):
    zeros = (0,) * len(shape)
    return pl.BlockSpec(shape, lambda *_: zeros, pipeline_mode=pl.Buffered(1))


def rows(height, width):
    return pl.BlockSpec((height, width), lambda i: (i, 0))


def standardize(v):
    average = jnp.mean(v, axis=-1, keepdims=True)
    centred = v - average
    variance = jnp.mean(centred * centred, axis=-1, keepdims=True)
    scale = lax.rsqrt(variance + EPSILON)
    return centred * scale, scale


def norm_backward(grad, gain, unit, scale):
    weighted = grad * gain
    first = jnp.mean(weighted, axis=-1, keepdims=True)
    second = jnp.mean(weighted * unit, axis=-1, keepdims=True)
    return scale * (weighted - first - unit * second)


def dot(a, b, contract):
    return lax.dot_general(a, b, ((contract[:1], contract[1:]), ((), ())), preferred_element_type=F32)


def fold(v):
    return jnp.sum(v.reshape(v.shape[0] // 8, 8, v.shape[1]), axis=0)


def project_body(x_ref, w_ref, vec_ref, out_ref):
    width = x_ref.shape[1]
    unit, _ = standardize(x_ref[...].astype(F32))
    normed = (unit * vec_ref[0:1, :] + vec_ref[1:2, :]).astype(BF)
    q = dot(normed, w_ref[:, :width], (1, 0)) + vec_ref[2:3, :]
    out_ref[:, :width] = (q * HEAD_DIM**-0.5).astype(BF)
    out_ref[:, width : 2 * width] = dot(normed, w_ref[:, width : 2 * width], (1, 0)).astype(BF)
    v = dot(normed, w_ref[:, 2 * width :], (1, 0)) + vec_ref[3:4, :]
    out_ref[:, 2 * width :] = v.astype(BF)


def project(x, w, vec):
    count, width = x.shape
    height = 512
    return pl.pallas_call(
        project_body,
        grid=(count // height,),
        in_specs=[rows(height, width), whole(w.shape), whole(vec.shape)],
        out_specs=rows(height, w.shape[1]),
        out_shape=jax.ShapeDtypeStruct((count, w.shape[1]), BF),
        compiler_params=params(),
        cost_estimate=cost(2 * count * w.size, 2 * (x.size + w.size + count * w.shape[1])),
        name="project",
    )(x, w, vec)


def key_span(lens_ref, seq, tile, tiles):
    length = lens_ref[seq, 0]
    total = tiles * TILE
    first = tile * TILE
    last = first + TILE - 1
    start = jnp.where(first < length, 0, length)
    end_one = jnp.minimum(((last >> 8) + 1) << 8, length)
    end_two = jnp.minimum(length + ((((last - length) >> 8) + 1) << 8), total)
    end = jnp.where(last < length, end_one, end_two)
    low = start >> 7
    high = (end + TILE - 1) >> 7
    count = jnp.maximum(high - low, 2)
    low = jnp.minimum(low, tiles - count)
    return low, count


def fill_bias(lens_ref, bias_ref, seq, tiles):
    length = lens_ref[seq, 0]
    total = tiles * TILE

    def one(tile, carry):
        low, count = key_span(lens_ref, seq, tile, tiles)
        query = tile * TILE + lax.broadcasted_iota(jnp.int32, (1, TILE), 1)
        early = query < length
        start = jnp.where(early, 0, length)
        end_one = jnp.minimum(((query >> 8) + 1) << 8, length)
        end_two = jnp.minimum(length + ((((query - length) >> 8) + 1) << 8), total)
        end = jnp.where(early, end_one, end_two)
        key = low * TILE + lax.broadcasted_iota(jnp.int32, (total, 1), 0)
        seen = (key >= start) & (key < end)
        bias_ref[tile] = jnp.where(seen, 0.0, MASKED_SCORE)
        return carry

    lax.fori_loop(0, tiles, one, 0)


def split_heads(v):
    lane = lax.broadcasted_iota(jnp.int32, v.shape, 1)
    zero = jnp.zeros_like(v)
    return jnp.concatenate(
        [jnp.where(lane < HEAD_DIM, v, zero), jnp.where(lane < HEAD_DIM, zero, v)], axis=0
    )


def join_heads(v):
    return jnp.concatenate([v[:HEAD_DIM, :TILE], v[HEAD_DIM:, TILE:]], axis=0)


def attend_body(lens_ref, q_ref, k_ref, v_ref, o_ref, lse_ref, bias_ref, vt_ref):
    seq, pair = pl.program_id(0), pl.program_id(1)
    tiles = q_ref.shape[0] // TILE

    @pl.when(pair == 0)
    def _():
        fill_bias(lens_ref, bias_ref, seq, tiles)

    vt_ref[...] = v_ref[...].T

    def one(tile, carry):
        low, count = key_span(lens_ref, seq, tile, tiles)
        at = pl.multiple_of(low * TILE, TILE)
        here = pl.multiple_of(tile * TILE, TILE)

        def variant(blocks):
            size = blocks * TILE
            q = split_heads(q_ref[pl.ds(here, TILE), :])
            scores = dot(k_ref[pl.ds(at, size), :], q, (1, 1))
            bias = bias_ref[tile, :size, :]
            scores = scores + jnp.concatenate([bias, bias], axis=1)
            top = jnp.max(scores, axis=0, keepdims=True)
            exponent = jnp.exp(scores - top)
            total = jnp.sum(exponent, axis=0, keepdims=True)
            mixed = dot(vt_ref[:, pl.ds(at, size)], exponent.astype(BF), (1, 0)) / total
            o_ref[pl.ds(here, TILE), :] = join_heads(mixed).T
            lse_ref[0, pl.ds(tile, 1), :] = top + jnp.log(total)

        for blocks in range(2, tiles + 1):
            pl.when(count == blocks)(functools.partial(variant, blocks))
        return carry

    lax.fori_loop(0, tiles, one, 0)


def attend(lens, qkv, length):
    count = qkv.shape[0]
    seqs = count // length
    pairs = HEADS // 2
    tiles = length // TILE
    take = lambda part: pl.BlockSpec((length, TILE), lambda s, p, *_: (s, part * pairs + p))
    grid_spec = pltpu.PrefetchScalarGridSpec(
        num_scalar_prefetch=1,
        grid=(seqs, pairs),
        in_specs=[take(0), take(1), take(2)],
        out_specs=[
            pl.BlockSpec((length, TILE), lambda s, p, *_: (s, p)),
            pl.BlockSpec((1, tiles, 2 * TILE), lambda s, p, *_: (s * pairs + p, 0, 0)),
        ],
        scratch_shapes=[pltpu.VMEM((tiles, length, TILE), F32), pltpu.VMEM((TILE, length), BF)],
    )
    return pl.pallas_call(
        attend_body,
        grid_spec=grid_spec,
        out_shape=[
            jax.ShapeDtypeStruct((count, HEADS * HEAD_DIM), F32),
            jax.ShapeDtypeStruct((seqs * pairs, tiles, 2 * TILE), F32),
        ],
        compiler_params=params(),
        cost_estimate=cost(12 * count * length * HEADS * HEAD_DIM, 12 * count * HEADS * HEAD_DIM),
        name="attend",
    )(lens, qkv, qkv, qkv)


def attend_back_body(
    lens_ref, q_ref, k_ref, v_ref, g_ref, lse_ref, inner_ref,
    dq_ref, dk_ref, dv_ref, sum_ref, bias_ref, kt_ref, dk_acc, dv_acc, row_ref,
):
    seq, pair = pl.program_id(0), pl.program_id(1)
    tiles = q_ref.shape[0] // TILE

    @pl.when(pair == 0)
    def _():
        fill_bias(lens_ref, bias_ref, seq, tiles)

    for head in range(2):
        line = inner_ref[pl.ds(2 * pair + head, 1), :]
        for tile in range(tiles):
            row_ref[tile : tile + 1, head * TILE : (head + 1) * TILE] = line[
                :, tile * TILE : (tile + 1) * TILE
            ]
    kt_ref[...] = k_ref[...].T
    dk_acc[...] = jnp.zeros_like(dk_acc)
    dv_acc[...] = jnp.zeros_like(dv_acc)

    def one(tile, carry):
        low, count = key_span(lens_ref, seq, tile, tiles)
        at = pl.multiple_of(low * TILE, TILE)
        here = pl.multiple_of(tile * TILE, TILE)

        def variant(blocks):
            size = blocks * TILE
            q = split_heads(q_ref[pl.ds(here, TILE), :])
            g = split_heads(g_ref[pl.ds(here, TILE), :])
            scores = dot(k_ref[pl.ds(at, size), :], q, (1, 1))
            bias = bias_ref[tile, :size, :]
            scores = scores + jnp.concatenate([bias, bias], axis=1)
            weights = jnp.exp(scores - lse_ref[0, pl.ds(tile, 1), :])
            grad = dot(v_ref[pl.ds(at, size), :], g, (1, 1))
            ds = (weights * (grad - row_ref[pl.ds(tile, 1), :])).astype(BF)
            dv_acc[pl.ds(at, size), :] += dot(weights.astype(BF), g, (1, 0))
            dk_acc[pl.ds(at, size), :] += dot(ds, q, (1, 0))
            dq = join_heads(dot(kt_ref[:, pl.ds(at, size)], ds, (1, 0))).T
            dq_ref[pl.ds(here, TILE), :] = (dq * HEAD_DIM**-0.5).astype(BF)

        for blocks in range(2, tiles + 1):
            pl.when(count == blocks)(functools.partial(variant, blocks))
        return carry

    lax.fori_loop(0, tiles, one, 0)
    dk_ref[...] = dk_acc[...].astype(BF)
    dv_ref[...] = dv_acc[...].astype(BF)
    sum_ref[0, 0:1, :] = jnp.sum(dq_ref[...].astype(F32), axis=0, keepdims=True)
    sum_ref[0, 1:2, :] = jnp.sum(dk_ref[...].astype(F32), axis=0, keepdims=True)
    sum_ref[0, 2:3, :] = jnp.sum(dv_ref[...].astype(F32), axis=0, keepdims=True)


def attend_back(lens, qkv, grads, lse, inner, length):
    count = qkv.shape[0]
    seqs = count // length
    pairs = HEADS // 2
    tiles = length // TILE
    width = HEADS * HEAD_DIM
    take = lambda part: pl.BlockSpec((length, TILE), lambda s, p, *_: (s, part * pairs + p))
    grid_spec = pltpu.PrefetchScalarGridSpec(
        num_scalar_prefetch=1,
        grid=(seqs, pairs),
        in_specs=[
            take(0), take(1), take(2), take(0),
            pl.BlockSpec((1, tiles, 2 * TILE), lambda s, p, *_: (s * pairs + p, 0, 0)),
            pl.BlockSpec((inner.shape[0], length), lambda s, p, *_: (0, s)),
        ],
        out_specs=[
            take(0), take(0), take(0),
            pl.BlockSpec((1, 8, TILE), lambda s, p, *_: (s, 0, p)),
        ],
        scratch_shapes=[
            pltpu.VMEM((tiles, length, TILE), F32),
            pltpu.VMEM((TILE, length), BF),
            pltpu.VMEM((length, TILE), F32),
            pltpu.VMEM((length, TILE), F32),
            pltpu.VMEM((tiles, 2 * TILE), F32),
        ],
    )
    return pl.pallas_call(
        attend_back_body,
        grid_spec=grid_spec,
        out_shape=[jax.ShapeDtypeStruct((count, width), BF)] * 3
        + [jax.ShapeDtypeStruct((seqs, 8, width), F32)],
        compiler_params=params(),
        cost_estimate=cost(30 * count * length * width, 14 * count * width),
        name="attend_back",
    )(lens, qkv, qkv, qkv, grads, lse, inner)


def middle_one_body(
    o_ref, x_ref, wo_ref, w1_ref, vec_ref, wide_ref,
    a_ref, x1_ref, h2_ref, a2_ref, unit_ref, slope_ref, act_ref, der_ref,
):
    unit, _ = standardize(o_ref[...])
    a = (unit * vec_ref[0:1, :] + vec_ref[1:2, :]).astype(BF)
    a_ref[...] = a
    x1 = x_ref[...].astype(F32) + dot(a, wo_ref[...], (1, 0)) + vec_ref[2:3, :]
    x1_ref[...] = x1
    unit, _ = standardize(x1)
    h2 = (unit * vec_ref[3:4, :] + vec_ref[4:5, :]).astype(BF)
    h2_ref[...] = h2
    height, hidden = act_ref.shape
    part = 512
    total = jnp.zeros((height, 128), F32)
    for start in range(0, hidden, part):
        cols = slice(start, start + part)
        f = dot(h2, w1_ref[:, cols], (1, 0)) + wide_ref[0:1, cols]
        cdf = 0.5 * (1.0 + lax.erf(f * 0.7071067811865476))
        pdf = 0.3989422804014327 * jnp.exp(-0.5 * f * f)
        act = f * cdf
        act_ref[:, cols] = act
        der_ref[:, cols] = cdf + f * pdf
        for at in range(0, part, 128):
            total = total + act[:, at : at + 128]
    average = jnp.sum(total, axis=-1, keepdims=True) / hidden
    total = jnp.zeros((height, 128), F32)
    for start in range(0, hidden, 128):
        centred = act_ref[:, start : start + 128] - average
        total = total + centred * centred
    scale = lax.rsqrt(jnp.sum(total, axis=-1, keepdims=True) / hidden + EPSILON)
    for start in range(0, hidden, part):
        cols = slice(start, start + part)
        unit = (act_ref[:, cols] - average) * scale
        unit_ref[:, cols] = unit.astype(BF)
        a2_ref[:, cols] = (unit * wide_ref[1:2, cols] + wide_ref[2:3, cols]).astype(BF)
        slope_ref[:, cols] = (der_ref[:, cols] * scale).astype(BF)


def middle_one(o, x, wo, w1, vec, wide):
    count, width = x.shape
    hidden = w1.shape[1]
    height = 256
    return pl.pallas_call(
        middle_one_body,
        grid=(count // height,),
        in_specs=[
            rows(height, width), rows(height, width), whole(wo.shape), whole(w1.shape),
            whole(vec.shape), whole(wide.shape),
        ],
        out_specs=[rows(height, width)] * 3 + [rows(height, hidden)] * 3,
        out_shape=[
            jax.ShapeDtypeStruct((count, width), BF),
            jax.ShapeDtypeStruct((count, width), F32),
            jax.ShapeDtypeStruct((count, width), BF),
        ]
        + [jax.ShapeDtypeStruct((count, hidden), BF)] * 3,
        scratch_shapes=[pltpu.VMEM((height, hidden), F32)] * 2,
        compiler_params=params(),
        cost_estimate=cost(2 * count * (wo.size + w1.size), 6 * count * hidden, 2 * count * hidden),
        name="middle_one",
    )(o, x, wo, w1, vec, wide)


def middle_two_body(
    a2_ref, unit_ref, slope_ref, x1_ref, e_ref, o_ref, w2_ref, w1_ref, wo_ref, vec_ref, wide_ref,
    out_ref, df_ref, dx1_ref, dr_ref, do_ref, inner_ref, sums_ref, wsums_ref, grad_ref,
):
    @pl.when(pl.program_id(0) == 0)
    def _():
        sums_ref[...] = jnp.zeros_like(sums_ref)
        wsums_ref[...] = jnp.zeros_like(wsums_ref)

    height, hidden = grad_ref.shape
    part = 512
    x1 = x1_ref[...]
    e = e_ref[...]
    e_wide = e.astype(F32)
    out_ref[...] = (x1 + dot(a2_ref[...], w2_ref[...], (1, 0)) + vec_ref[5:6, :]).astype(BF)
    sums_ref[0] += fold(e_wide)
    first = jnp.zeros((height, 128), F32)
    second = jnp.zeros((height, 128), F32)
    for start in range(0, hidden, part):
        cols = slice(start, start + part)
        grad = dot(e, w2_ref[cols, :], (1, 1))
        unit = unit_ref[:, cols].astype(F32)
        wsums_ref[0, :, cols] += fold(grad)
        wsums_ref[1, :, cols] += fold(grad * unit)
        grad = grad * wide_ref[1:2, cols]
        grad_ref[:, cols] = grad
        scaled = grad * unit
        for at in range(0, part, 128):
            first = first + grad[:, at : at + 128]
            second = second + scaled[:, at : at + 128]
    first = jnp.sum(first, axis=-1, keepdims=True) / hidden
    second = jnp.sum(second, axis=-1, keepdims=True) / hidden
    dh2 = jnp.zeros_like(x1)
    for start in range(0, hidden, part):
        cols = slice(start, start + part)
        unit = unit_ref[:, cols].astype(F32)
        df = ((grad_ref[:, cols] - first - unit * second) * slope_ref[:, cols].astype(F32)).astype(BF)
        df_ref[:, cols] = df
        wsums_ref[2, :, cols] += fold(df.astype(F32))
        dh2 = dh2 + dot(df, w1_ref[:, cols], (1, 1))
    unit, scale = standardize(x1)
    sums_ref[1] += fold(dh2 * unit)
    sums_ref[2] += fold(dh2)
    dx1 = e_wide + norm_backward(dh2, vec_ref[3:4, :], unit, scale)
    dx1_ref[...] = dx1
    dr = dx1.astype(BF)
    dr_ref[...] = dr
    sums_ref[3] += fold(dr.astype(F32))
    da = dot(dr, wo_ref[...], (1, 1))
    o = o_ref[...]
    unit, scale = standardize(o)
    sums_ref[4] += fold(da * unit)
    sums_ref[5] += fold(da)
    do = norm_backward(da, vec_ref[0:1, :], unit, scale).astype(BF)
    do_ref[...] = do
    product = do.astype(F32) * o
    high = product.astype(BF)
    low = (product - high.astype(F32)).astype(BF)
    head = lax.broadcasted_iota(jnp.int32, (16, product.shape[1]), 0)
    lane = lax.broadcasted_iota(jnp.int32, (16, product.shape[1]), 1)
    pick = jnp.where((lane >= head * HEAD_DIM) & (lane < (head + 1) * HEAD_DIM), 1.0, 0.0).astype(BF)
    inner_ref[...] = dot(pick, high, (1, 1)) + dot(pick, low, (1, 1))


def middle_two(a2, unit, slope, x1, e, o, w2, w1, wo, vec, wide):
    count, width = x1.shape
    hidden = w1.shape[1]
    height = 256
    return pl.pallas_call(
        middle_two_body,
        grid=(count // height,),
        in_specs=[rows(height, hidden)] * 3
        + [rows(height, width)] * 3
        + [whole(v.shape) for v in (w2, w1, wo, vec, wide)],
        out_specs=[
            rows(height, width), rows(height, hidden), rows(height, width), rows(height, width),
            rows(height, width),
            pl.BlockSpec((16, height), lambda i: (0, i)),
            pl.BlockSpec((6, 8, width), lambda i: (0, 0, 0)),
            pl.BlockSpec((3, 8, hidden), lambda i: (0, 0, 0)),
        ],
        out_shape=[
            jax.ShapeDtypeStruct((count, width), BF),
            jax.ShapeDtypeStruct((count, hidden), BF),
            jax.ShapeDtypeStruct((count, width), F32),
            jax.ShapeDtypeStruct((count, width), BF),
            jax.ShapeDtypeStruct((count, width), BF),
            jax.ShapeDtypeStruct((16, count), F32),
            jax.ShapeDtypeStruct((6, 8, width), F32),
            jax.ShapeDtypeStruct((3, 8, hidden), F32),
        ],
        scratch_shapes=[pltpu.VMEM((height, hidden), F32)],
        compiler_params=params(),
        cost_estimate=cost(2 * count * (wo.size + 3 * w1.size), 10 * count * hidden),
        name="middle_two",
    )(a2, unit, slope, x1, e, o, w2, w1, wo, vec, wide)


def input_body(dq_ref, dk_ref, dv_ref, x_ref, dx1_ref, w_ref, vec_ref, out_ref, sums_ref):
    @pl.when(pl.program_id(0) == 0)
    def _():
        sums_ref[...] = jnp.zeros_like(sums_ref)

    width = x_ref.shape[1]
    du = dot(dq_ref[...], w_ref[:, :width], (1, 1))
    du = du + dot(dk_ref[...], w_ref[:, width : 2 * width], (1, 1))
    du = du + dot(dv_ref[...], w_ref[:, 2 * width :], (1, 1))
    unit, scale = standardize(x_ref[...].astype(F32))
    sums_ref[0] += fold(du * unit)
    sums_ref[1] += fold(du)
    out_ref[...] = (dx1_ref[...] + norm_backward(du, vec_ref[0:1, :], unit, scale)).astype(BF)


def input_gradient(dq, dk, dv, x, dx1, w, vec):
    count, width = x.shape
    height = 512
    return pl.pallas_call(
        input_body,
        grid=(count // height,),
        in_specs=[rows(height, width)] * 5 + [whole(w.shape), whole(vec.shape)],
        out_specs=[rows(height, width), pl.BlockSpec((2, 8, width), lambda i: (0, 0, 0))],
        out_shape=[
            jax.ShapeDtypeStruct((count, width), BF),
            jax.ShapeDtypeStruct((2, 8, width), F32),
        ],
        compiler_params=params(),
        cost_estimate=cost(2 * count * w.size, 14 * count * width),
        name="input_gradient",
    )(dq, dk, dv, x, dx1, w, vec)


def renorm_body(x_ref, vec_ref, out_ref):
    unit, _ = standardize(x_ref[...].astype(F32))
    out_ref[...] = (unit * vec_ref[0:1, :] + vec_ref[1:2, :]).astype(BF)


def renorm(x, vec):
    count, width = x.shape
    height = 512
    return pl.pallas_call(
        renorm_body,
        grid=(count // height,),
        in_specs=[rows(height, width), whole(vec.shape)],
        out_specs=rows(height, width),
        out_shape=jax.ShapeDtypeStruct((count, width), BF),
        compiler_params=params(),
        name="renorm",
    )(x, vec)


def gather(shard, columns):
    return lax.all_gather(shard.reshape(-1, columns), "fsdp", axis=0, tiled=True)


def scatter(grad):
    return lax.psum_scatter(grad, "fsdp", scatter_dimension=0, tiled=True).astype(F32).reshape(-1)


def weight_gradient(a, b):
    return dot(a, b, (0, 0)).astype(BF)


def shards(hidden_in, doc_lens, w_qkv, w_out, w_fc1, w_fc2, vec_params, cotangent):
    micro_count, length, width = hidden_in.shape
    count = micro_count * length
    devices = lax.axis_size("fsdp")
    hidden = w_fc1.shape[0] * devices // width
    x = hidden_in.reshape(count, width)
    e = cotangent.reshape(count, width)
    lens = doc_lens.reshape(micro_count, doc_lens.shape[-1])

    vector = lax.all_gather(
        jnp.pad(vec_params, (0, -vec_params.shape[0] % 1024)).reshape(1, -1), "fsdp", axis=0, tiled=True
    )[:, : vec_params.shape[0]].reshape(-1).astype(F32)
    qkv_w = gather(w_qkv, 3 * width)
    out_w = gather(w_out, width)
    fc1_w = gather(w_fc1, hidden)
    fc2_w = gather(w_fc2, width)
    narrow = vector[: 9 * width].reshape(9, width)
    wide = vector[9 * width : 9 * width + 3 * hidden].reshape(3, hidden)
    last = vector[9 * width + 3 * hidden :].reshape(1, width)
    vec_one = narrow[0:4]
    vec_mid = jnp.concatenate([narrow[4:9], last], axis=0)

    qkv = project(x, qkv_w, vec_one)
    o, lse = attend(lens, qkv, length)
    a, x1, h2, a2, unit, slope = middle_one(o, x, out_w, fc1_w, vec_mid, wide)
    grad_fc2 = weight_gradient(a2, e)
    out, df, dx1, dr, do, inner, sums, wsums = middle_two(
        a2, unit, slope, x1, e, o, fc2_w, fc1_w, out_w, vec_mid, wide
    )
    grad_fc1 = weight_gradient(h2, df)
    grad_out = weight_gradient(a, dr)
    dq, dk, dv, bias_sums = attend_back(lens, qkv, do, lse, inner, length)
    normed = renorm(x, vec_one)
    grad_qkv = weight_gradient(normed, jnp.concatenate([dq, dk, dv], axis=1))
    grad_in, in_sums = input_gradient(dq, dk, dv, x, dx1, qkv_w, vec_one)

    sums = jnp.sum(sums, axis=1)
    wsums = jnp.sum(wsums, axis=1)
    in_sums = jnp.sum(in_sums, axis=1)
    bias_sums = jnp.sum(bias_sums, axis=0)
    grad_vec = jnp.concatenate(
        [
            in_sums[0], in_sums[1], bias_sums[0], bias_sums[2], sums[4], sums[5], sums[3], sums[1],
            sums[2], wsums[2], wsums[1], wsums[0], sums[0],
        ]
    )
    grad_vec = grad_vec.reshape(devices, -1)
    kept = grad_vec.shape[1]
    grad_vec = jnp.pad(grad_vec, ((0, 0), (0, -kept % 1024)))
    vec_share = lax.psum_scatter(grad_vec, "fsdp", scatter_dimension=0, tiled=True)[0, :kept]
    return (
        out.reshape(hidden_in.shape),
        grad_in.reshape(hidden_in.shape),
        scatter(grad_qkv),
        scatter(grad_out),
        scatter(grad_fc1),
        scatter(grad_fc2),
        vec_share,
    )


def solution(mesh):
    return jax.shard_map(
        shards,
        mesh=mesh,
        in_specs=(
            P(None, "fsdp", None),
            P(None, "fsdp", None),
            P("fsdp"),
            P("fsdp"),
            P("fsdp"),
            P("fsdp"),
            P("fsdp"),
            P(None, "fsdp", None),
        ),
        out_specs=(
            P(None, "fsdp", None),
            P(None, "fsdp", None),
            P("fsdp"),
            P("fsdp"),
            P("fsdp"),
            P("fsdp"),
            P("fsdp"),
        ),
        check_vma=False,
    )
```

time: 1680 us -> 985 us (0.59)
  matrix products: 823 us -> 49.8 us
  Pallas kernels: 0 us -> 277 us
  other arithmetic: 172 us -> 2.51 us
  local copies, waits for them, and re-layouts: 149 us -> 20.4 us
  waiting for transfers between devices: 465 us -> 567 us
    dot_general x48 -> x4, matrix products: 823 us -> 49.8 us  [dot(): lax.dot_general(a, b, ((contract[:1], contract[1:]), ((), ())), preferred...]
    reduce_scatter x0 -> x4, waiting for transfers between devices: none -> 425 us  [scatter(): lax.psum_scatter(grad, 'fsdp', scatter_dimension=0, tiled=True).astype(F32)]
    unnamed x6 -> x10, waiting for transfers between devices: 413 us -> 65.5 us
    pallas_call x0 -> x7, Pallas kernels: none -> 277 us  [the longest x1 68.3 us: attend_back(): pl.pallas_call(attend_back_body, grid_spec=grid_spec, out_shape=[jax.Shap...]
    reduce_sum x32 -> x4, other arithmetic: 150 us -> 0.96 us  [the longest x1 0.82 us: shards(): in_sums = jnp.sum(in_sums, axis=1)]
    unnamed x390 -> x23, local copies, waits for them, and re-layouts: 51.2 us -> 4.52 us
    all_gather x0 -> x1, blocking collectives: none -> 43.5 us  [shards(): lax.all_gather(jnp.pad(vec_params, (0, -vec_params.shape[0] % 1024)).resh...]
    unnamed x1 -> x0, blocking collectives: 42.4 us -> none
  transfers between devices with their start and end apart: 5 -> 9, of which waited for: 2 -> 8; matrix products, arithmetic and copies ran while one was open for 20% -> 7% of each run, Pallas kernels for 0% -> 13%
where the time goes in v1:
time: 985 us; the launch traced here: 976 us
  waiting for transfers between devices  567 us (58%)
  Pallas kernels  277 us (28%)
  matrix products  49.8 us (5%)
  blocking collectives  43.5 us (4%)
  local copies, waits for them, and re-layouts  20.4 us (2%)
  between operations  14.6 us (1%)
    reduce_scatter x4, waiting for transfers between devices, scatter(): lax.psum_scatter(grad, 'fsdp', scatter_dimension=0, tiled=True).astype(F32)  425 us
    all_gather x4, waiting for transfers between devices, gather(): lax.all_gather(shard.reshape(-1, columns), 'fsdp', axis=0, tiled=True)  76.6 us
    pallas_call x1, Pallas kernels, attend_back(): pl.pallas_call(attend_back_body, grid_spec=grid_spec, out_shape=[jax.Shap...  68.3 us
    pallas_call x1, Pallas kernels, attend(): pl.pallas_call(attend_body, grid_spec=grid_spec, out_shape=[jax.ShapeDtyp...  67.9 us
    unnamed x10, waiting for transfers between devices  65.5 us
    pallas_call x1, Pallas kernels, middle_two(): pl.pallas_call(middle_two_body, grid=(count // height,), in_specs=[rows(h...  62.4 us
    dot_general x4, matrix products, dot(): lax.dot_general(a, b, ((contract[:1], contract[1:]), ((), ())), preferred...  49.8 us
    pallas_call x1, Pallas kernels, middle_one(): pl.pallas_call(middle_one_body, grid=(count // height,), in_specs=[rows(h...  44.8 us
  transfers between devices with their start and end apart: 9, of which 8 were waited for; matrix products, arithmetic and copies ran while one was open for 7% of the time, Pallas kernels for 13%

profile of v1, /device:TPU:0, one launch (start us, length us, event | category | flops | bytes accessed | tf_op | source)
XLA Modules:
  0.0 976.1 jit_solution(10145200524146401414)
XLA Ops:
  7.2 0.0 all-gather.6.cloned.1.call-start
  7.2 1.7 reshape.95
  8.9 0.0 all-gather.6.cloned.1.call-update
  8.9 0.0 all-gather.8.cloned.1.call-start
  9.0 1.4 reshape.97
  10.4 0.0 all-gather.8.cloned.1.call-update
  10.4 0.0 all-gather.10.cloned.1.call-start
  10.5 1.6 reshape.98
  12.1 0.0 all-gather.10.cloned.1.call-update
  12.2 0.0 all-gather.12.cloned.1.call-start
  12.2 1.7 reshape.102
  13.9 0.0 all-gather.12.cloned.1.call-update
  13.9 0.0 all-reduce.5.cloned.1.call-start
  14.0 0.7 pad.8
  14.7 43.5 %all-gather = bf16[32768]{0:T(1024)(128)(2,1)S(1)} all-gather(bf16[1024]{0:T(1024)(128)(2,1)S(1)} %pad.8), channel_id=2, replica_groups=mesh['fsdp'=32] {'fsdp'}, dimensions={0}, use_global_device_ids=true | all-gather | bytes 67584 | tf_op jit(solution)/shard_map/all_gather | solution.py:528
  58.3 0.1 reshape.114
  58.4 0.6 slice.88.vec_ref
  59.0 0.1 reshape.115
  59.1 0.6 reshape.100.wide_ref
  59.8 0.6 pad_maximum_fusion.vec_ref
  60.4 13.9 %all-gather.6.cloned.1.call-done.w_ref = bf16[768,2304]{1,0:T(8,128)(2,1)} async-done(((bf16[24,2304]{1,0:T(8,128)(2,1)}), bf16[768,2304]{1,0:T(8,128)(2,1)}) %all-gather.6.cloned.1.call-update) | async-done | bytes 3538960 | tf_op jit(solution)/shard_map/all_gather | solution.py:508
  74.3 13.2 %project.1.q_ref.k_ref.v_ref = bf16[2048,2304]{1,0:T(8,128)(2,1)} custom-call(bf16[2048,768]{1,0:T(8,128)(2,1)} %bitcast.18, bf16[768,2304]{1,0:T(8,128)(2,1)} %all-gather.6.cloned.1.call-done.w_ref, f32[4,768]{1,0:T(4,128)} %slice.88.vec_ref), custom_call_target="tpu_custom_call" | custom-call | flops 7247757312 | bytes 16121856 | tf_op jit(solution)/shard_map/project/pallas_call | solution.py:78
  87.5 67.9 %attend.1 = (f32[2048,768]{1,0:T(8,128)}, f32[12,8,256]{2,1,0:T(8,128)}) custom-call(s32[2,2]{1,0:T(2,128)} %bitcast.28, bf16[2048,2304]{1,0:T(8,128)(2,1)} %project.1.q_ref.k_ref.v_ref, bf16[2048,2304]{1,0:T(8,128)(2,1)} %project.1.q_ref.k_ref.v_ref, bf16[2048,2304]{1,0:T(8,128)(2,1)} %project.1.q_ref.k_ref.v_ref), custom_call_target="tpu_custom_call" | custom-call | flops 19327352832 | bytes 18874368 | tf_op jit(solution)/shard_map/attend/pallas_call | solution.py:189
  155.4 41.6 %all-gather.10.cloned.1.call-done.w1_ref = bf16[768,3072]{1,0:T(8,128)(2,1)} async-done(((bf16[24,3072]{1,0:T(8,128)(2,1)}), bf16[768,3072]{1,0:T(8,128)(2,1)}) %all-gather.10.cloned.1.call-update) | async-done | bytes 4718608 | tf_op jit(solution)/shard_map/all_gather | solution.py:508
  197.0 44.8 %middle_one.1 = (bf16[2048,768]{1,0:T(8,128)(2,1)}, f32[2048,768]{1,0:T(8,128)}, bf16[2048,768]{1,0:T(8,128)(2,1)}, bf16[2048,3072]{1,0:T(8,128)(2,1)}, bf16[204...) custom-call(f32[2048,768]{1,0:T(8,128)} %get-tuple-element.29.o_ref, bf16[2048,768]{1,0:T(8,128)(2,1)} %bitcast.19, ...), custom_call_target="tpu_custom_call" | custom-call | flops 12079595520 | bytes 37748736 | tf_op jit(solution)/shard_map/middle_one/pallas_call | solution.py:336
  241.8 21.0 %all-gather.12.cloned.1.call-done.w2_ref = bf16[3072,768]{1,0:T(8,128)(2,1)} async-done(((bf16[96,768]{1,0:T(8,128)(2,1)}), bf16[3072,768]{1,0:T(8,128)(2,1)}) %all-gather.12.cloned.1.call-update) | async-done | bytes 4718608 | tf_op jit(solution)/shard_map/all_gather | solution.py:508
  262.8 62.4 %middle_two.1 = (bf16[2048,768]{1,0:T(8,128)(2,1)}, bf16[2048,3072]{1,0:T(8,128)(2,1)}, f32[2048,768]{1,0:T(8,128)}, bf16[2048,768]{1,0:T(8,128)(2,1)}, bf16[204...) custom-call(bf16[2048,3072]{1,0:T(8,128)(2,1)} %get-tuple-element.30.a2_ref, ...), custom_call_target="tpu_custom_call" | custom-call | flops 31406948352 | bytes 62914560 | tf_op jit(solution)/shard_map/middle_two/pallas_call | solution.py:425
  325.2 68.3 %attend_back.1 = (bf16[2048,768]{1,0:T(8,128)(2,1)}, bf16[2048,768]{1,0:T(8,128)(2,1)}, bf16[2048,768]{1,0:T(8,128)(2,1)}, f32[2,8,768]{2,1,0:T(8,128)}) custom-call(s32[2,2]{1,0:T(2,128)} %bitcast.29, bf16[2048,2304]{1,0:T(8,128)(2,1)} %project.1.q_ref.k_ref.v_ref, bf16[2048,2304]{1,0:T(8,128)(2,1)} %project.1.q_ref.k_ref.v_ref, ...), custom_call_target="tpu_custom_call" | custom-call | flops 48318382080 | bytes 22020096 | tf_op jit(solution)/shard_map/attend_back/pallas_call | solution.py:282
  393.6 0.0 copy-start.1
  393.6 0.0 copy-start
  393.6 15.7 %input_gradient.1 = (bf16[2048,768]{1,0:T(8,128)(2,1)}, f32[2,8,768]{2,1,0:T(8,128)}) custom-call(bf16[2048,768]{1,0:T(8,128)(2,1)} %get-tuple-element.38.dq_ref, bf16[2048,768]{1,0:T(8,128)(2,1)} %get-tuple-element.39.dk_ref, bf16[2048,768]{1,0:T(8,128)(2,1)} %get-tuple-element.40.dv_ref, bf16[2048,768]{1,0:T(8,128)(2,1)} %bitcast.20, ...), custom_call_target="tpu_custom_call" | custom-call | flops 7247757312 | bytes 22020096 | tf_op jit(solution)/shard_map/input_gradient/pallas_call | solution.py:473
  409.2 0.8 reduce_sum.36
  410.1 0.0 copy-done.1
  410.2 0.1 slice_reduce_fusion
  410.3 0.1 reduce_sum.39
  410.6 0.1 reshape.113
  410.7 0.7 pad.9
  411.3 0.0 all-reduce.5.cloned.1.call-update
  411.4 0.0 reduce-scatter.7.cloned.1.call-start
  411.4 6.6 convolution_convert_fusion.2
  418.0 0.0 reduce-scatter.7.cloned.1.call-update
  418.0 0.0 reduce-scatter.5.cloned.1.call-start
  418.1 5.3 renorm.1
  423.3 14.0 %fusion.6 = bf16[768,2304]{1,0:T(8,128)(2,1)} fusion(bf16[2048,768]{1,0:T(8,128)(2,1)} %renorm.1, bf16[2048,768]{1,0:T(8,128)(2,1)} %get-tuple-element.40.dv_ref, bf16[2048,768]{1,0:T(8,128)(2,1)} %get-tuple-element.39.dk_ref, bf16[2048,768]{1,0:T(8,128)(2,1)} %get-tuple-element.38.dq_ref), kind=kOutput, calls=%fused_computation.8 | convolution fusion | flops 7277838336 | bytes 16121856 | tf_op jit(solution)/shard_map/dot_general | solution.py:57
  437.4 0.0 reduce-scatter.5.cloned.1.call-update
  437.4 0.0 reduce-scatter.9.cloned.1.call-start
  437.4 1.8 copy-done.4
  439.3 14.7 %convolution_convert_fusion.1 = bf16[768,3072]{1,0:T(8,128)(2,1)} fusion(bf16[2048,768]{1,0:T(8,128)(2,1)S(1)} %copy-done.4, bf16[2048,3072]{1,0:T(8,128)(2,1)} %get-tuple-element.46), kind=kOutput, calls=%fused_computation.7 | convolution fusion | flops 9666035712 | bytes 20447232 | tf_op jit(solution)/shard_map/dot_general | solution.py:57
  454.0 0.0 reduce-scatter.9.cloned.1.call-update
  454.0 0.0 reduce-scatter.11.cloned.1.call-start
  454.1 1.8 copy-done.3
  455.9 14.5 %convolution_convert_fusion = bf16[3072,768]{1,0:T(8,128)(2,1)} fusion(bf16[2048,3072]{1,0:T(8,128)(2,1)} %get-tuple-element.30.a2_ref, bf16[2048,768]{1,0:T(8,128)(2,1)S(1)} %bitcast.27), kind=kOutput, calls=%fused_computation.6 | convolution fusion | flops 9666035712 | bytes 20447232 | tf_op jit(solution)/shard_map/dot_general | solution.py:57
  470.4 0.0 reduce-scatter.11.cloned.1.call-update
  470.4 65.4 %all-reduce.5.cloned.1.call-done = f32[32,1024]{1,0:T(8,128)} async-done(((f32[32,1024]{1,0:T(8,128)}), f32[32,1024]{1,0:T(8,128)}) %all-reduce.5.cloned.1.call-update) | async-done | bytes 131088
  535.8 1.3 dynamic-slice_reduce_fusion
  537.1 98.8 %reduce-scatter.7.cloned.1.call-done = bf16[24,768]{1,0:T(8,128)(2,1)} async-done(((bf16[768,768]{1,0:T(8,128)(2,1)}), bf16[24,768]{1,0:T(8,128)(2,1)}) %reduce-scatter.7.cloned.1.call-update) | async-done | bytes 36880 | tf_op jit(solution)/shard_map/reduce_scatter | solution.py:512
  636.0 1.4 reshape.119
  637.4 106.0 %reduce-scatter.5.cloned.1.call-done = bf16[24,2304]{1,0:T(8,128)(2,1)} async-done(((bf16[768,2304]{1,0:T(8,128)(2,1)}), bf16[24,2304]{1,0:T(8,128)(2,1)}) %reduce-scatter.5.cloned.1.call-update) | async-done | bytes 110608 | tf_op jit(solution)/shard_map/reduce_scatter | solution.py:512
  743.4 1.7 reshape.117
  745.1 109.8 %reduce-scatter.9.cloned.1.call-done = bf16[24,3072]{1,0:T(8,128)(2,1)} async-done(((bf16[768,3072]{1,0:T(8,128)(2,1)}), bf16[24,3072]{1,0:T(8,128)(2,1)}) %reduce-scatter.9.cloned.1.call-update) | async-done | bytes 147472 | tf_op jit(solution)/shard_map/reduce_scatter | solution.py:512
  854.9 0.9 convert_bitcast_fusion
  855.8 0.8 copy.15
  856.6 110.8 %reduce-scatter.11.cloned.1.call-done = bf16[96,768]{1,0:T(8,128)(2,1)} async-done(((bf16[3072,768]{1,0:T(8,128)(2,1)}), bf16[96,768]{1,0:T(8,128)(2,1)}) %reduce-scatter.11.cloned.1.call-update) | async-done | bytes 147472 | tf_op jit(solution)/shard_map/reduce_scatter | solution.py:512
  967.4 1.8 reshape.123
  (31 shorter events, 0.3 us)
Async XLA Ops:
  7.2 67.1 %all-gather.6.cloned.1.call-start = ((), (), s32[]{:S(2)}) async-start(), calls=%async_computation.4 | async-start | bytes 3649536 | tf_op jit(solution)/shard_map/all_gather | solution.py:508
  8.9 146.4 %all-gather.8.cloned.1.call-start = ((), (), s32[]{:S(2)}) async-start(), calls=%async_computation.5 | async-start | bytes 1216512 | tf_op jit(solution)/shard_map/all_gather | solution.py:508
  10.4 186.5 %all-gather.10.cloned.1.call-start = ((), (), s32[]{:S(2)}) async-start(), calls=%async_computation.6 | async-start | bytes 4866048 | tf_op jit(solution)/shard_map/all_gather | solution.py:508
  12.2 250.7 %all-gather.12.cloned.1.call-start = ((), (), s32[]{:S(2)}) async-start(), calls=%async_computation.7 | async-start | bytes 4866048 | tf_op jit(solution)/shard_map/all_gather | solution.py:508
  13.9 521.8 %all-reduce.5.cloned.1.call-start = ((), (), s32[]{:S(2)}) async-start(), calls=%async_computation.12 | async-start | bytes 262144
  393.5 16.5 %copy-start.2 = (f32[2,8,768]{2,1,0:T(8,128)S(1)}, f32[2,8,768]{2,1,0:T(8,128)}, u32[]{:S(2)}) copy-start(f32[2,8,768]{2,1,0:T(8,128)} %get-tuple-element.48) | copy-start | bytes 147460
  393.6 16.6 %copy-start.1 = (f32[6,8,768]{2,1,0:T(8,128)S(1)}, f32[6,8,768]{2,1,0:T(8,128)}, u32[]{:S(2)}) copy-start(f32[6,8,768]{2,1,0:T(8,128)} %get-tuple-element.49) | copy-start | bytes 442372
  393.6 16.7 %copy-start = (f32[3,8,3072]{2,1,0:T(8,128)S(1)}, f32[3,8,3072]{2,1,0:T(8,128)}, u32[]{:S(2)}) copy-start(f32[3,8,3072]{2,1,0:T(8,128)} %get-tuple-element.50) | copy-start | bytes 884740
  411.4 224.6 %reduce-scatter.7.cloned.1.call-start = ((), (), s32[]{:S(2)}) async-start(), calls=%async_computation.9 | async-start | bytes 1216512 | tf_op jit(solution)/shard_map/reduce_scatter | solution.py:512
  418.0 325.4 %reduce-scatter.5.cloned.1.call-start = ((), (), s32[]{:S(2)}) async-start(), calls=%async_computation.8 | async-start | bytes 3649536 | tf_op jit(solution)/shard_map/reduce_scatter | solution.py:512
  437.4 1.9 copy-start.4
  437.4 417.5 %reduce-scatter.9.cloned.1.call-start = ((), (), s32[]{:S(2)}) async-start(), calls=%async_computation.10 | async-start | bytes 4866048 | tf_op jit(solution)/shard_map/reduce_scatter | solution.py:512
  454.0 1.9 copy-start.3
  454.0 513.4 %reduce-scatter.11.cloned.1.call-start = ((), (), s32[]{:S(2)}) async-start(), calls=%async_computation.11 | async-start | bytes 4866048 | tf_op jit(solution)/shard_map/reduce_scatter | solution.py:512
Sparse Core Ops, SparseCore 0:
  11.5 62.7 all-gather.5
  77.8 53.0 all-gather.7
  134.3 62.6 all-gather.9
  200.3 62.4 all-gather.11
  411.5 124.2 all-reduce.4
  540.7 95.1 reduce-scatter.6
  641.4 101.9 reduce-scatter.4
  748.9 105.9 reduce-scatter.8
  861.3 106.0 reduce-scatter.10
